TPU v7x, 256 devices: a whole 4x4x8 slice. The times are simulated.
256 devices in a mesh: grp: 2 (over z_lo), dp: 32 (over y, z_hi, core), mp: 4 (over x).
Axes of the slice: x: 4, y: 4, z: 8 (z_hi: 4, z_lo: 2; z = z_hi * 2 + z_lo), core: 2. Of those that a mesh axis runs over, the one named last changes fastest.
Arguments:
- up_input: bfloat16 [64, 256, 4096], P(('grp', 'dp'), None, 'mp'), may hold values from -6 to 6
- gate_pre: bfloat16 [64, 256, 14336], P(('grp', 'dp'), None, 'mp'), may hold values from -6 to 6
- up_pre: bfloat16 [64, 256, 14336], P(('grp', 'dp'), None, 'mp'), may hold values from -6 to 6
- grad_hidden: bfloat16 [64, 256, 14336], P(('grp', 'dp'), None, 'mp'), may hold values from -6 to 6
- grad_output: bfloat16 [64, 256, 4096], P(('grp', 'dp'), None, 'mp'), may hold values from -6 to 6
- proj_up_in: bfloat16 [64, 4096], P(None, 'mp'), may hold values from -0.09375 to 0.09375
- proj_up_out: bfloat16 [64, 14336], P(None, 'mp'), may hold values from -0.046875 to 0.046875
- proj_down_in: bfloat16 [64, 14336], P(None, 'mp'), may hold values from -0.046875 to 0.046875
- proj_down_out: bfloat16 [64, 4096], P(None, 'mp'), may hold values from -0.09375 to 0.09375
- gram: float32 [8192, 8192], P(('grp', 'mp'), 'dp'), may hold values from -4 to 14
- canaries: bfloat16 [1024, 8192], P('dp', ('grp', 'mp')), may hold values from -6 to 6
Outputs:
- gram_new: float32 [8192, 8192], P(('grp', 'mp'), 'dp')
- mapped: bfloat16 [1024, 8192], P(('grp', 'mp'), 'dp')
- scores: float32 [64, 1024], P(None, ('grp', 'mp'))
All inputs are finite; a program needn't handle non-finite values.
Results may differ from a plain program's by a relative error of at most 0.005.
Values may be sent and summed in bfloat16 or wider, within the bound.
A program may use at most 64 MiB of HBM per device.

v0:
```python
import math

import jax
import jax.numpy as jnp
from jax import lax
from jax.sharding import Mesh
from jax.sharding import PartitionSpec as P

GRP_DP = ("grp", "dp_0", "dp_1", "dp_2")
DP = ("dp_0", "dp_1", "dp_2")


def sent_to_all(shard, axis):
    devices = lax.axis_size(axis)
    return lax.all_to_all(
        jnp.broadcast_to(shard[None], (devices, *shard.shape)), axis, 0, 0, tiled=True
    )


def taken_together(shard, axis):
    everything = sent_to_all(shard, axis)
    return jnp.sum(everything, axis=0)


def in_one(arrays, axis):
    ends = [0]
    for a in arrays:
        ends.append(ends[-1] + a.size)
    subtotal = taken_together(jnp.concatenate([a.ravel() for a in arrays]), axis)
    return tuple((subtotal[b:e].reshape(a.shape) for a, b, e in zip(arrays, ends, ends[1:])))


def in_order(parts, dim):
    lengths = list(parts.shape[1:])
    lengths[dim] *= parts.shape[0]
    return jnp.moveaxis(parts, 0, dim).reshape(lengths)


def whole_of(shard, axes, dim):
    far, near = axes
    parts = sent_to_all(sent_to_all(shard, far), near)
    return in_order(parts.swapaxes(0, 1).reshape(-1, *shard.shape), dim)


def split_up(shard, dim, devices):
    before, after = (shard.shape[:dim], shard.shape[dim + 1 :])
    return jnp.moveaxis(shard.reshape(*before, devices, -1, *after), dim, 0)


def sum_at_owner(shard, axis, dim):
    parts = split_up(shard, dim, lax.axis_size(axis))
    arrived = lax.all_to_all(parts, axis, split_axis=0, concat_axis=0, tiled=True)
    return arrived.sum(axis=0)


def project(values, matrix):
    return lax.dot_general(
        values, matrix, (((1,), (1,)), ((), ())), preferred_element_type=jnp.float32
    )


def shards(
    up_input,
    gate_pre,
    up_pre,
    grad_hidden,
    grad_output,
    proj_up_in,
    proj_up_out,
    proj_down_in,
    proj_down_out,
    gram,
    canaries,
):
    seq_len = up_input.shape[1]
    gate_act = jax.nn.silu(gate_pre[0].astype(jnp.float32))
    grad_up = (grad_hidden[0].astype(jnp.float32) * gate_act).astype(jnp.bfloat16)
    hidden = (gate_act * up_pre[0].astype(jnp.float32)).astype(jnp.bfloat16)
    in_up, out_up, in_down, out_down = in_one(
        (
            project(up_input[0], proj_up_in),
            project(grad_up, proj_up_out),
            project(hidden, proj_down_in),
            project(grad_output[0], proj_down_out),
        ),
        "mp",
    )
    norm_len = 1.0 / math.sqrt(seq_len)
    up_feat = jnp.dot(out_up.T, in_up, precision=lax.Precision.HIGHEST) * norm_len
    down_feat = jnp.dot(out_down.T, in_down, precision=lax.Precision.HIGHEST) * norm_len
    own_row = jnp.concatenate([up_feat.reshape(-1), down_feat.reshape(-1)])[None, :]
    feature_rows = whole_of(own_row, (("grp", "dp_0", "dp_1"), "dp_2"), 0)
    seq_total = feature_rows.shape[0]
    feature_count = feature_rows.shape[1]
    rows_here = gram.shape[0]
    cols_here = gram.shape[1]
    block_row = lax.axis_index("grp") * lax.axis_size("mp") + lax.axis_index("mp")
    block_col = lax.axis_index(DP)
    left_block = lax.dynamic_slice_in_dim(feature_rows, block_row * rows_here, rows_here, 1)
    right_block = lax.dynamic_slice_in_dim(feature_rows, block_col * cols_here, cols_here, 1)
    gram_new = (
        gram + jnp.dot(left_block.T, right_block, precision=lax.Precision.HIGHEST) / seq_total
    )
    gram_low = gram_new.astype(jnp.bfloat16)
    norm_order = 1.0 / math.sqrt(feature_count)
    gathered = lax.all_gather(canaries, DP, axis=0, tiled=True)
    mapped_share = (
        sum_at_owner(
            jnp.dot(gathered, gram_low, preferred_element_type=jnp.float32), ("grp", "mp"), 0
        )
        * norm_order
    )
    scores = taken_together(
        jnp.dot(right_block, mapped_share.T, precision=lax.Precision.HIGHEST) * norm_order, DP
    )
    return (gram_new, mapped_share.astype(jnp.bfloat16), scores)


def solution(mesh):
    finer = Mesh(
        mesh.devices.reshape(mesh.shape["grp"], 4, 4, 2, mesh.shape["mp"]),
        ("grp", "dp_0", "dp_1", "dp_2", "mp"),
    )
    in_specs = (
        P(GRP_DP, None, "mp"),
        P(GRP_DP, None, "mp"),
        P(GRP_DP, None, "mp"),
        P(GRP_DP, None, "mp"),
        P(GRP_DP, None, "mp"),
        P(None, "mp"),
        P(None, "mp"),
        P(None, "mp"),
        P(None, "mp"),
        P(("grp", "mp"), DP),
        P(DP, ("grp", "mp")),
    )
    out_specs = (P(("grp", "mp"), DP), P(("grp", "mp"), DP), P(None, ("grp", "mp")))
    return jax.shard_map(
        shards, mesh=finer, in_specs=in_specs, out_specs=out_specs, check_vma=False
    )
```

profile of v0, /device:TPU:1, one launch (start us, length us, event | category | flops | bytes accessed | tf_op | source)
XLA Modules:
  0.0 167.7 jit_solution(15573984106864743045)
XLA Ops:
  7.2 0.0 copy-start
  7.2 1.0 copy-done
  8.2 1.2 fusion.14
  9.4 0.1 reshape.82
  9.5 0.0 copy-start.4
  9.5 3.4 %fusion.5 = f32[256,64]{1,0:T(8,128)S(1)} fusion(bf16[64,3584]{1,0:T(8,128)(2,1)} %param.17, bf16[1,256,3584]{2,1,0:T(8,128)(2,1)} %param.14, bf16[1,256,3584]{2,1,0:T(8,128)(2,1)} %param.12), kind=kOutput, calls=%fused_computation.9 | convolution fusion | flops 124780544 | bytes 4194304 | tf_op jit(solution)/shard_map/dot_general | solution.py:57
  12.9 0.1 reshape.83
  13.0 0.0 copy-start.2
  13.0 0.0 copy-start.3
  13.1 2.8 %fusion.7 = f32[256,64]{1,0:T(8,128)S(1)} fusion(bf16[64,3584]{1,0:T(8,128)(2,1)} %param.18, bf16[1,256,3584]{2,1,0:T(8,128)(2,1)S(1)} %copy-done.4, bf16[1,256,3584]{2,1,0:T(8,128)(2,1)} %param.12), kind=kOutput, calls=%fused_computation.10 | convolution fusion | flops 124780544 | bytes 4194304 | tf_op jit(solution)/shard_map/dot_general | solution.py:57
  15.9 0.1 reshape.84
  16.0 0.0 copy-done.2
  16.0 0.3 fusion.12
  16.3 0.1 reshape.85
  16.4 1.5 broadcast_in_dim.10
  17.9 4.8 %all-to-all-start = ((f32[4,1,65536]{2,1,0:T(1,128)}), f32[4,1,65536]{2,1,0:T(1,128)S(1)}, u32[]{:S(2)}, u32[]{:S(2)}) async-start(f32[4,1,65536]{2,1,0:T(1,128)} %broadcast_in_dim.10), calls=%async_computation | async-start | bytes 2097152 | tf_op jit(solution)/shard_map/all_to_all | solution.py:15
  22.7 0.7 all-gather.2.cloned.1.call-update
  23.4 12.6 %all-to-all-done = f32[4,1,65536]{2,1,0:T(1,128)S(1)} async-done(((f32[4,1,65536]{2,1,0:T(1,128)}), f32[4,1,65536]{2,1,0:T(1,128)S(1)}, u32[]{:S(2)}, u32[]{:S(2)}) %all-to-all-start) | async-done | bytes 1048608 | tf_op jit(solution)/shard_map/all_to_all | solution.py:15
  36.1 1.0 reduce_sum.27
  37.0 0.1 slice.53
  37.1 0.1 slice.55
  37.2 0.4 convolution_multiply_fusion.3
  37.6 0.1 reshape.86
  37.7 0.1 slice.57
  37.8 0.1 slice.59
  37.8 0.4 convolution_multiply_fusion.2
  38.2 0.1 reshape.87
  38.3 1.9 %broadcast_in_dim.11 = f32[32,1,8192]{2,1,0:T(1,128)} broadcast(f32[8192]{0:T(1024)S(1)} %pad_maximum_fusion.1), dimensions={2} | broadcast | bytes 1081344 | tf_op jit(solution)/shard_map/broadcast_in_dim | solution.py:16
  40.2 12.1 %all-to-all-start.1 = ((f32[32,1,8192]{2,1,0:T(1,128)}), f32[32,1,8192]{2,1,0:T(1,128)S(1)}, u32[]{:S(2)}, u32[]{:S(2)}) async-start(f32[32,1,8192]{2,1,0:T(1,128)} %broadcast_in_dim.11), calls=%async_computation.1 | async-start | bytes 2097152 | tf_op jit(solution)/shard_map/all_to_all | solution.py:15
  52.4 28.3 %all-to-all-done.1 = f32[32,1,8192]{2,1,0:T(1,128)S(1)} async-done(((f32[32,1,8192]{2,1,0:T(1,128)}), f32[32,1,8192]{2,1,0:T(1,128)S(1)}, u32[]{:S(2)}, u32[]{:S(2)}) %all-to-all-start.1) | async-done | bytes 1048608 | tf_op jit(solution)/shard_map/all_to_all | solution.py:15
  80.6 0.6 copy.58
  81.3 0.1 broadcast_in_dim.13
  81.4 13.5 %all_to_all.26 = f32[2,32,1,8192]{3,1,2,0:T(8,128)S(1)} all-to-all(f32[2,32,1,8192]{3,1,2,0:T(8,128)S(1)} %broadcast_in_dim.13), channel_id=1, replica_groups=mesh['grp'=2,'dp_0'=4,'dp_1'=4,'dp_2'=2,'mp'=4] {'dp_2'}, dimensions={0} | all-to-all | bytes 4194304 | tf_op jit(solution)/shard_map/all_to_all | solution.py:15
  94.9 1.6 copy.39
  96.5 2.5 %reshape_reshape.3 = f32[64,8192]{1,0:T(8,128)} reshape(f32[32,2,1,8192]{3,1,0,2:T(2,128)S(1)} %copy.39) | data formatting | bytes 4194304 | tf_op jit(solution)/shard_map/reshape;reshape | solution.py:36
  98.9 2.4 %fusion.11 = f32[1024,256]{1,0:T(8,128)S(1)} fusion(f32[1024,256]{1,0:T(8,128)} %param.20, f32[64,8192]{1,0:T(8,128)} %reshape_reshape.3, s32[]{:T(128)S(6)} %select_n.6, s32[]{:T(128)S(6)} %select_n.7), kind=kOutput, calls=%fused_computation.15 | convolution fusion | flops 201850880 | bytes 2424840 | tf_op jit(solution)/shard_map/dot_general | solution.py:102
  101.3 0.0 copy-start.1
  101.3 0.0 all-gather.2.cloned.1.call-done
  101.4 2.7 %convolution_bitcast_fusion = f32[32,8,8,128]{3,2,1,0:T(8,128)S(1)} fusion(bf16[1024,1024]{1,0:T(8,128)(2,1)} %all-gather.2.cloned.1.call-done, f32[1024,256]{1,0:T(8,128)S(1)} %fusion.11), kind=kOutput, calls=%fused_computation.13 | convolution fusion | flops 537133056 | bytes 4194304 | tf_op jit(solution)/shard_map/dot_general | solution.py:109
  104.1 0.1 copy.57
  104.2 17.1 %all_to_all.27 = f32[8,128,256]{1,2,0:T(8,128)S(1)} all-to-all(f32[8,128,256]{1,2,0:T(8,128)S(1)} %bitcast.50), channel_id=1, replica_groups=mesh['grp'=2,'dp_0'=4,'dp_1'=4,'dp_2'=2,'mp'=4] {'grp','mp'}, dimensions={0} | all-to-all | bytes 2097152 | tf_op jit(solution)/shard_map/all_to_all | solution.py:52
  121.3 0.1 reduce_sum.28
  121.4 1.1 convolution_multiply_fusion.1
  122.4 1.1 broadcast_in_dim.14
  123.5 7.9 %all-to-all-start.4 = ((f32[32,64,128]{2,1,0:T(8,128)}), f32[32,64,128]{2,1,0:T(8,128)S(1)}, u32[]{:S(2)}, u32[]{:S(2)}) async-start(f32[32,64,128]{2,1,0:T(8,128)} %broadcast_in_dim.14), calls=%async_computation.4 | async-start | bytes 2097152 | tf_op jit(solution)/shard_map/all_to_all | solution.py:15
  131.4 0.7 copy.42
  132.2 28.0 %all-to-all-done.4 = f32[32,64,128]{2,1,0:T(8,128)S(1)} async-done(((f32[32,64,128]{2,1,0:T(8,128)}), f32[32,64,128]{2,1,0:T(8,128)S(1)}, u32[]{:S(2)}, u32[]{:S(2)}) %all-to-all-start.4) | async-done | bytes 1048608 | tf_op jit(solution)/shard_map/all_to_all | solution.py:15
  160.2 0.7 reduce_sum.29
  (8 shorter events, 0.1 us)
Async XLA Ops:
  7.2 1.0 copy-start
  9.5 3.5 %copy-start.4 = (bf16[1,256,3584]{2,1,0:T(8,128)(2,1)S(1)}, bf16[1,256,3584]{2,1,0:T(8,128)(2,1)}, u32[]{:S(2)}) copy-start(bf16[1,256,3584]{2,1,0:T(8,128)(2,1)} %param.13) | copy-start | bytes 5505028
  13.0 2.9 %copy-start.2 = (bf16[1,256,1024]{2,1,0:T(8,128)(2,1)S(1)}, bf16[1,256,1024]{2,1,0:T(8,128)(2,1)}, u32[]{:S(2)}) copy-start(bf16[1,256,1024]{2,1,0:T(8,128)(2,1)} %param.15) | copy-start | bytes 1572868
  13.0 2.9 %copy-start.3 = (bf16[64,1024]{1,0:T(8,128)(2,1)S(1)}, bf16[64,1024]{1,0:T(8,128)(2,1)}, u32[]{:S(2)}) copy-start(bf16[64,1024]{1,0:T(8,128)(2,1)} %param.19) | copy-start | bytes 393220
  17.9 18.2 %all-to-all-start = ((f32[4,1,65536]{2,1,0:T(1,128)}), f32[4,1,65536]{2,1,0:T(1,128)S(1)}, u32[]{:S(2)}, u32[]{:S(2)}) async-start(f32[4,1,65536]{2,1,0:T(1,128)} %broadcast_in_dim.10), calls=%async_computation | async-start | bytes 2097152 | tf_op jit(solution)/shard_map/all_to_all | solution.py:15
  22.7 78.6 %all-gather.2.cloned.1.call-start = ((), (), s32[]{:S(2)}) async-start(), calls=%async_computation.5 | async-start | bytes 2162688 | tf_op jit(solution)/shard_map/all_gather | solution.py:106
  40.2 40.4 %all-to-all-start.1 = ((f32[32,1,8192]{2,1,0:T(1,128)}), f32[32,1,8192]{2,1,0:T(1,128)S(1)}, u32[]{:S(2)}, u32[]{:S(2)}) async-start(f32[32,1,8192]{2,1,0:T(1,128)} %broadcast_in_dim.11), calls=%async_computation.1 | async-start | bytes 2097152 | tf_op jit(solution)/shard_map/all_to_all | solution.py:15
  101.3 2.8 %copy-start.1 = (f32[1024,256]{1,0:T(8,128)}, f32[1024,256]{1,0:T(8,128)S(1)}, u32[]{:S(2)}) copy-start(f32[1024,256]{1,0:T(8,128)S(1)} %fusion.11) | copy-start | bytes 3145732
  123.5 36.7 %all-to-all-start.4 = ((f32[32,64,128]{2,1,0:T(8,128)}), f32[32,64,128]{2,1,0:T(8,128)S(1)}, u32[]{:S(2)}, u32[]{:S(2)}) async-start(f32[32,64,128]{2,1,0:T(8,128)} %broadcast_in_dim.14), calls=%async_computation.4 | async-start | bytes 2097152 | tf_op jit(solution)/shard_map/all_to_all | solution.py:15
Sparse Core Ops, SparseCore 0:
  26.1 64.1 all-gather.1
where the time goes:
time: 168 us
  waiting for transfers between devices  69.6 us (41%)
  blocking collectives  30.6 us (18%)
  starting transfers between devices  24.8 us (15%)
  matrix products  14.6 us (9%)
  between operations  14.3 us (9%)
  local copies, waits for them, and re-layouts  12.1 us (7%)
  other arithmetic  1.74 us (1%)
    all_to_all x3, waiting for transfers between devices, sent_to_all(): lax.all_to_all(jnp.broadcast_to(shard[None], (devices, *shard.shape)), ax...  68.9 us
    all_to_all x3, starting transfers between devices, sent_to_all(): lax.all_to_all(jnp.broadcast_to(shard[None], (devices, *shard.shape)), ax...  24.8 us
    all_to_all x1, blocking collectives, sum_at_owner(): lax.all_to_all(parts, axis, split_axis=0, concat_axis=0, tiled=True)  17.1 us
    all_to_all x1, blocking collectives, sent_to_all(): lax.all_to_all(jnp.broadcast_to(shard[None], (devices, *shard.shape)), ax...  13.5 us
    dot_general x4, matrix products, project(): lax.dot_general(values, matrix, (((1,), (1,)), ((), ())), preferred_eleme...  7.69 us
    broadcast_in_dim x4, local copies, waits for them, and re-layouts, sent_to_all(): jnp.broadcast_to(shard[None], (devices, *shard.shape))  4.66 us
  transfers between devices with their start and end apart: 4, of which 3 were waited for; matrix products, arithmetic and copies ran while one was open for 7% of the time, Pallas kernels for 0%

commit v1 on v0

v1 whole, which is shorter than its diff:
```python
import functools
import math

import jax
import jax.numpy as jnp
from jax import lax
from jax.experimental import pallas as pl
from jax.experimental.pallas import tpu as pltpu
from jax.sharding import Mesh
from jax.sharding import PartitionSpec as P

GRP_DP = ("g", "y", "h", "c")
DP = ("y", "h", "c")
GX = ("g", "x")
NCH = 7
ROWS = 32
HI = lax.Precision.HIGHEST
F32 = jnp.float32
BF = jnp.bfloat16
NT = (((1,), (1,)), ((), ()))
TN = (((0,), (0,)), ((), ()))

C_Z, C_Y, C_P = 0, 4, 20
A_, FZ, FY, FK, FD, PX, PZ, TX, TZ, EZ, EY, EC = 36, 42, 49, 52, 53, 60, 66, 67, 70, 71, 74, 77
SLOTS = 78


def dot_nt(a, b, precision=None):
    return lax.dot_general(a, b, NT, precision=precision, preferred_element_type=F32)


def body(
    ui, gp, up, gh, go, pui, puo, pdi, pdo, gram, can,
    gram_out, mapped_out, scores_out,
    ui_v, gp_v, up_v, gh_v, go_v, pui_v, puo_v, pdi_v, pdo_v, gram_v,
    gu_b, hid_b, acc_ou, acc_id, gram_b,
    cf, a_in, a_out, ra_in, ra_out, fz, fall, fd,
    pst, pown, rp, qst, qown, rq, ts, town, rt, tq, rtq,
    es, res, ey, rey, ec, rec, r_v, t_v, k_v,
    ls, ss, rs, fdr,
):
    g, y, h, c, x = (lax.axis_index(n) for n in ("g", "y", "h", "c", "x"))
    z = h * 2 + g
    oc = 1 - c
    og = 1 - g

    def rem(v, n):
        return lax.rem(v, n)

    bar = pltpu.get_barrier_semaphore()

    def greet(**dev):
        pl.semaphore_signal(bar, inc=1, device_id=dev, device_id_type=pl.DeviceIdType.MESH)

    for r in range(1, 4):
        greet(x=rem(x + r, 4))
        greet(x=rem(x + r, 4), c=oc)
        greet(y=rem(y + r, 4))
    for r in range(1, 8):
        zz = rem(z + r, 8)
        greet(h=zz // 2, g=rem(zz, 2))
    greet(c=oc)

    loads = []

    def load(src, dst):
        cp = pltpu.make_async_copy(src, dst, ls.at[len(loads)])
        cp.start()
        loads.append(cp)
        return cp

    blk = lambda yy, hh, cc: (yy * 4 + hh) * 2 + cc
    l_c = load(can, cf.at[blk(y, h, c)])
    l_ch = []
    l_puo = load(puo, puo_v)
    l_pdi = load(pdi, pdi_v)
    for k in range(NCH):
        s = pl.ds(k * 512, 512)
        l_ch.append([load(a.at[0, :, s], b.at[k]) for a, b in ((gp, gp_v), (gh, gh_v), (up, up_v))])
    l_in = [load(a, b) for a, b in ((pui, pui_v), (ui.at[0], ui_v), (pdo, pdo_v), (go.at[0], go_v))]
    l_g = load(gram, gram_v)

    sent = []

    def rcopy(src, dst, slot, **dev):
        return pltpu.make_async_remote_copy(
            src_ref=src, dst_ref=dst, send_sem=ss.at[slot], recv_sem=rs.at[slot],
            device_id=dev, device_id_type=pl.DeviceIdType.MESH,
        )

    live = {}

    def send(src, dst, slot, **dev):
        cp = rcopy(src, dst, slot, **dev)
        cp.start()
        live[slot] = cp

    def got(slot):
        live[slot].wait_recv()

    def chunk(k):
        for cp in l_ch[k]:
            cp.wait()
        if k == 0:
            l_puo.wait()
            l_pdi.wait()

        def tile(i, _):
            rows = pl.ds(i * ROWS, ROWS)
            v = gp_v[k, rows, :].astype(F32)
            act = v / (1.0 + jnp.exp(-v))
            gu_b[rows, :] = (gh_v[k, rows, :].astype(F32) * act).astype(BF)
            hid_b[rows, :] = (act * up_v[k, rows, :].astype(F32)).astype(BF)
            return 0

        lax.fori_loop(0, 256 // ROWS, tile, 0)
        s = slice(k * 512, (k + 1) * 512)
        ou = dot_nt(puo_v[:, s], gu_b[...])
        idn = dot_nt(pdi_v[:, s], hid_b[...])
        if k == 0:
            acc_ou[...] = ou
            acc_id[...] = idn
        else:
            acc_ou[...] += ou
            acc_id[...] += idn

    hp, hm, h2 = rem(h + 1, 4), rem(h + 3, 4), rem(h + 2, 4)
    yp, ym, y2 = rem(y + 1, 4), rem(y + 3, 4), rem(y + 2, 4)
    hk = (h, hm, hp, h2)
    yj = (y, ym, yp, y2)
    lo, hi = pl.ds(0, 16), pl.ds(16, 16)

    def whole(b):
        return cf.at[b]

    def partner(j, k):
        b = blk(yj[j], hk[k], c)
        send(whole(b), whole(b), C_P + j * 4 + k, c=oc)

    def spread(k):
        b = blk(y, hk[k], c)
        send(whole(b), whole(b), C_Y + k, y=yp)
        send(whole(b), whole(b), C_Y + 4 + k, y=ym)
        partner(0, k)

    def c_start():
        b = blk(y, h, c)
        l_c.wait()
        send(whole(b), whole(b), C_Z, h=hp)
        send(whole(b), whole(b), C_Z + 1, h=hm)
        spread(0)

    def c_z1():
        got(C_Z)
        b = blk(y, hm, c)
        send(cf.at[b, lo], cf.at[b, lo], C_Z + 2, h=hp)
        spread(1)
        got(C_Z + 1)
        b = blk(y, hp, c)
        send(cf.at[b, hi], cf.at[b, hi], C_Z + 3, h=hm)
        spread(2)

    def c_z2():
        got(C_Z + 2)
        got(C_Z + 3)
        spread(3)

    def c_y1(k):
        got(C_Y + k)
        b = blk(ym, hk[k], c)
        send(cf.at[b, lo], cf.at[b, lo], C_Y + 8 + k, y=yp)
        partner(1, k)
        got(C_Y + 4 + k)
        b = blk(yp, hk[k], c)
        send(cf.at[b, hi], cf.at[b, hi], C_Y + 12 + k, y=ym)
        partner(2, k)

    def c_y2(k):
        got(C_Y + 8 + k)
        got(C_Y + 12 + k)
        partner(3, k)

    chunk(0)
    chunk(1)
    pl.semaphore_wait(bar, 17)
    c_start()
    for k in range(2, 5):
        chunk(k)
    c_z1()
    for k in range(5, NCH):
        chunk(k)
    for cp in l_in:
        cp.wait()
    iu = dot_nt(pui_v[...], ui_v[...])
    od = dot_nt(pdo_v[...], go_v[...])
    idn = acc_id[...]
    ou = acc_ou[...]

    a_in[0] = iu.astype(BF)
    a_in[1] = idn.astype(BF)
    a_out[:, 0] = ou.reshape(4, 16, 256)
    a_out[:, 1] = od.reshape(4, 16, 256)
    for r in range(1, 4):
        xp = rem(x + r, 4)
        send(a_in, ra_in.at[r - 1], A_ + 2 * (r - 1), x=xp)
        send(a_out.at[xp], ra_out.at[r - 1], A_ + 2 * (r - 1) + 1, x=xp)
    c_z2()
    l_g.wait()
    gram_b[...] = gram_v[...].astype(BF)

    lane = lax.broadcasted_iota(jnp.int32, (64, 1024), 1)
    tile_m = jnp.where(lane % 64 == lax.broadcasted_iota(jnp.int32, (64, 1024), 0), 1.0, 0.0).astype(BF)
    lane16 = lax.broadcasted_iota(jnp.int32, (16, 1024), 1)
    mask16 = lane16 // 64 == lax.broadcasted_iota(jnp.int32, (16, 1024), 0)

    for r in range(3):
        got(A_ + 2 * r)
        got(A_ + 2 * r + 1)
    for m, own in ((0, iu), (1, idn)):
        ins, outs = own, a_out[x, m]
        for r in range(3):
            ins = ins + ra_in[r, m].astype(F32)
            outs = outs + ra_out[r, m]
        feat = dot_nt(outs, ins, HI) * (1.0 / 16.0)
        spreadf = jnp.dot(feat.astype(BF), tile_m, preferred_element_type=F32)
        row = jnp.sum(jnp.where(mask16, spreadf, 0.0), axis=0, keepdims=True)
        fz[pl.ds(z, 1), m * 1024 : (m + 1) * 1024] = row

    for r in range(1, 8):
        zz = rem(z + r, 8)
        send(fz.at[pl.ds(z, 1)], fz.at[pl.ds(z, 1)], FZ + r - 1, h=zz // 2, g=rem(zz, 2))
    for k in range(4):
        c_y1(k)
    for r in range(7):
        got(FZ + r)
    fall[y, c] = fz[...].astype(BF)
    for r in range(1, 4):
        send(fall.at[y, c], fall.at[y, c], FY + r - 1, y=rem(y + r, 4))
    for k in range(4):
        c_y2(k)
    for j in range(4):
        for k in range(4):
            got(C_P + j * 4 + k)

    def rows_of(b):
        return cf[pl.ds(4 * b, 4)].reshape(128, 1024)

    def times_gram(b):
        return jnp.dot(rows_of(b), gram_b[...], preferred_element_type=F32)

    for r in range(1, 4):
        xp = rem(x + r, 4)
        for q in range(2):
            pst[r - 1, q] = times_gram(q * 4 + xp).astype(BF)
            send(pst.at[r - 1, q], rp.at[r - 1, q], PX + 2 * (r - 1) + q, x=xp)
    for r in range(3):
        got(FY + r)
    gl = pl.ds(pl.multiple_of(g * 1024, 1024), 1024)
    send(fall.at[:, c, :, gl], fall.at[:, c, :, gl], FK, c=oc)
    x_src = 2 * rem(y, 2) + h // 2
    base = (y // 2) * 1024 + rem(h, 2) * 512

    def fd_copies():
        def piece(cc):
            return fall.at[:, c, :, pl.ds(pl.multiple_of(base + cc * 256, 256), 256)]

        def to(i, cc, **dev):
            return pltpu.make_async_remote_copy(
                src_ref=piece(cc), dst_ref=fd.at[:, c], send_sem=ss.at[FD + i], recv_sem=fdr.at[c],
                device_id=dev, device_id_type=pl.DeviceIdType.MESH,
            )

        cps = []
        for r in range(1, 4):
            xp = rem(x + r, 4)
            cps.append(to(2 * r - 2, c, x=xp))
            cps.append(to(2 * r - 1, oc, x=xp, c=oc))
        cps.append(to(6, oc, c=oc))
        own = pltpu.make_async_copy(piece(c), fd.at[:, c], ls.at[len(loads)])
        return cps, own

    @pl.when(x == x_src)
    def _():
        cps, own = fd_copies()
        for cp in cps:
            cp.start()
        own.start()

    for q in range(2):
        pown[q] = times_gram(q * 4 + x)

    got(FK)
    fk32 = fall[:, :, :, gl].astype(F32).reshape(64, 1024)
    fk = fk32.astype(BF)
    ft = dot_nt(fk, cf[...].reshape(1024, 1024))
    fkk = dot_nt(fk, jnp.concatenate([fk, fk], axis=0))
    for b in range(8):
        town[b % 4, b // 4] = ft[:, b * 128 : (b + 1) * 128]
        ts[b % 4, b // 4] = ft[:, b * 128 : (b + 1) * 128].astype(BF)
    k_v[...] = fkk
    for b in range(4):
        ts[b, 2] = fkk.astype(BF)
    for r in range(1, 4):
        xp = rem(x + r, 4)
        send(ts.at[xp], rt.at[r - 1], TX + r - 1, x=xp)

    for r in range(6):
        got(PX + r)
    for q in range(2):
        acc = pown[q]
        for r in range(3):
            acc = acc + rp[r, q].astype(F32)
        qown[q] = acc
    qst[...] = qown[og].astype(BF)
    send(qst, rq, PZ, g=og)

    @pl.when(x == x_src)
    def _():
        cps, own = fd_copies()
        own.wait()

    @pl.when(x != x_src)
    def _():
        pltpu.make_async_remote_copy(
            src_ref=fd.at[:, c], dst_ref=fd.at[:, c], send_sem=ss.at[FD], recv_sem=fdr.at[c],
            device_id={"c": oc}, device_id_type=pl.DeviceIdType.MESH,
        ).wait_recv()

    pltpu.make_async_remote_copy(
        src_ref=fd.at[:, oc], dst_ref=fd.at[:, oc], send_sem=ss.at[FD], recv_sem=fdr.at[oc],
        device_id={"c": oc}, device_id_type=pl.DeviceIdType.MESH,
    ).wait_recv()
    fd32 = fd[...].astype(F32).reshape(64, 256)
    fdb = fd32.astype(BF)

    got(PZ)
    rr = qown[g] + rq[...].astype(F32)
    r_v[...] = rr
    r_hi = rr.astype(BF)
    r_lo = (rr - r_hi.astype(F32)).astype(BF)
    s1 = dot_nt(fdb, r_hi) + dot_nt(fdb, r_lo)
    ey[...] = s1
    es[...] = s1.astype(BF)
    for r in range(1, 4):
        send(es, res.at[r - 1], EZ + r - 1, h=rem(h + r, 4))

    for r in range(3):
        got(TX + r)
    for q in range(2):
        acc = town[x, q]
        for r in range(3):
            acc = acc + rt[r, q].astype(F32)
        town[x, q] = acc
    acc = k_v[...]
    for r in range(3):
        acc = acc + rt[r, 2].astype(F32)
    k_v[...] = acc
    tq[0] = town[x, og].astype(BF)
    tq[1] = acc.astype(BF)
    send(tq, rtq, TZ, g=og)

    for i in range(4):
        rows = slice(i * 256, (i + 1) * 256)
        gram_out[rows, :] = gram_v[rows, :] + lax.dot_general(
            fk[:, rows], fdb, TN, preferred_element_type=F32
        ) * (1.0 / 64.0)

    for r in range(3):
        got(EZ + r)
    acc = ey[...]
    for r in range(3):
        acc = acc + res[r].astype(F32)
    ec[...] = acc
    for r in range(1, 4):
        send(ec, rey.at[r - 1], EY + r - 1, y=rem(y + r, 4))

    got(TZ)
    t_f = town[x, g] + rtq[0].astype(F32)
    k_f = (k_v[...] + rtq[1].astype(F32))[:, :64]
    norm = 1.0 / math.sqrt(8192.0)
    tf = lax.dot_general(t_f, fd32, TN, precision=HI, preferred_element_type=F32)
    mapped_out[...] = ((r_v[...] + tf * (1.0 / 64.0)) * norm).astype(BF)
    kt = jnp.dot(k_f, t_f, precision=HI, preferred_element_type=F32)

    for r in range(3):
        got(EY + r)
    acc = ec[...]
    for r in range(3):
        acc = acc + rey[r]
    t_v[...] = acc
    send(t_v, rec, EC, c=oc)
    got(EC)
    total = (acc + rec[...] + kt * (1.0 / 64.0)) * (1.0 / 8192.0)
    for s in range(64):
        yy, cc, zz = s // 16, (s // 8) % 2, s % 8
        t = (zz % 2) * 32 + yy * 8 + (zz // 2) * 2 + cc
        scores_out[t : t + 1, :] = total[s : s + 1, :]

    for cp in live.values():
        cp.wait_send()

    @pl.when(x == x_src)
    def _():
        cps, own = fd_copies()
        for cp in cps:
            cp.wait_send()


def shards(*args):
    any_ = pl.BlockSpec(memory_space=pl.ANY)
    vm = pl.BlockSpec(memory_space=pltpu.VMEM)
    V = pltpu.VMEM
    scratch = [
        V((256, 1024), BF), V((NCH, 256, 512), BF), V((NCH, 256, 512), BF), V((NCH, 256, 512), BF),
        V((256, 1024), BF), V((64, 1024), BF), V((64, 3584), BF), V((64, 3584), BF), V((64, 1024), BF),
        V((1024, 256), F32),
        V((256, 512), BF), V((256, 512), BF), V((64, 256), F32), V((64, 256), F32), V((1024, 256), BF),
        V((32, 32, 1024), BF),
        V((2, 64, 256), BF), V((4, 2, 16, 256), F32), V((3, 2, 64, 256), BF), V((3, 2, 16, 256), F32),
        V((8, 2048), F32), V((4, 2, 8, 2048), BF), V((4, 2, 8, 256), BF),
        V((3, 2, 128, 256), BF), V((2, 128, 256), F32), V((3, 2, 128, 256), BF),
        V((128, 256), BF), V((2, 128, 256), F32), V((128, 256), BF),
        V((4, 3, 64, 128), BF), V((4, 2, 64, 128), F32), V((3, 3, 64, 128), BF),
        V((2, 64, 128), BF), V((2, 64, 128), BF),
        V((64, 128), BF), V((3, 64, 128), BF), V((64, 128), F32), V((3, 64, 128), F32),
        V((64, 128), F32), V((64, 128), F32), V((128, 256), F32), V((64, 128), F32), V((64, 128), F32),
        pltpu.SemaphoreType.DMA((40,)), pltpu.SemaphoreType.DMA((SLOTS,)), pltpu.SemaphoreType.DMA((SLOTS,)),
        pltpu.SemaphoreType.DMA((2,)),
    ]
    return pl.pallas_call(
        body,
        name="step",
        out_shape=(
            jax.ShapeDtypeStruct((1024, 256), F32),
            jax.ShapeDtypeStruct((128, 256), BF),
            jax.ShapeDtypeStruct((64, 128), F32),
        ),
        in_specs=[any_] * 11,
        out_specs=(vm, vm, vm),
        scratch_shapes=scratch,
        compiler_params=pltpu.CompilerParams(collective_id=0, has_side_effects=True),
    )(*args)


def solution(mesh):
    finer = Mesh(mesh.devices.reshape(2, 4, 4, 2, 4), ("g", "y", "h", "c", "x"))
    in_specs = (P(GRP_DP, None, "x"),) * 5 + (P(None, "x"),) * 4 + (P(GX, DP), P(DP, GX))
    out_specs = (P(GX, DP), P(GX, DP), P(None, GX))
    return jax.shard_map(shards, mesh=finer, in_specs=in_specs, out_specs=out_specs, check_vma=False)
```

time: 168 us -> 57.8 us (0.34)
  waiting for transfers between devices: 69.6 us -> 0 us
  Pallas kernels: 0 us -> 53.5 us
  blocking collectives: 30.6 us -> 0 us
  starting transfers between devices: 24.8 us -> 0 us
  matrix products: 14.6 us -> 0 us
  between operations: 14.3 us -> 0.66 us
  local copies, waits for them, and re-layouts: 12.1 us -> 3.55 us
  other arithmetic: 1.74 us -> 0 us
    all_to_all x3 -> x0, waiting for transfers between devices: 68.9 us -> none  [sent_to_all(): lax.all_to_all(jnp.broadcast_to(shard[None], (devices, *shard.shape)), ax...]
    pallas_call x0 -> x1, Pallas kernels: none -> 53.5 us  [shards(): pl.pallas_call(body, name='step', out_shape=(jax.ShapeDtypeStruct((1024,...]
    all_to_all x2 -> x0, blocking collectives: 30.6 us -> none  [the longest x1 17.1 us: sum_at_owner(): lax.all_to_all(parts, axis, split_axis=0, concat_axis=0, tiled=True)]
    all_to_all x3 -> x0, starting transfers between devices: 24.8 us -> none  [sent_to_all(): lax.all_to_all(jnp.broadcast_to(shard[None], (devices, *shard.shape)), ax...]
    dot_general x9 -> x0, matrix products: 14.6 us -> none  [the longest x4 7.69 us: project(): lax.dot_general(values, matrix, (((1,), (1,)), ((), ())), preferred_eleme...]
    broadcast_in_dim x4 -> x0, local copies, waits for them, and re-layouts: 4.66 us -> none  [sent_to_all(): jnp.broadcast_to(shard[None], (devices, *shard.shape))]
    another operation x1 -> x0, local copies, waits for them, and re-layouts: 2.46 us -> none  [in_order(): return jnp.moveaxis(parts, 0, dim).reshape(lengths)]
    reduce_sum x3 -> x0, other arithmetic: 1.7 us -> none  [the longest x2 1.64 us: taken_together(): return jnp.sum(everything, axis=0)]
  transfers between devices with their start and end apart: 4 -> 0, of which waited for: 3 -> 0; matrix products, arithmetic and copies ran while one was open for 7% -> 0% of each run, Pallas kernels for 0% -> 0%
where the time goes in v1:
time: 57.8 us; the launch traced here: 57.7 us
  Pallas kernels  53.5 us (93%)
  local copies, waits for them, and re-layouts  3.55 us (6%)
  between operations  0.66 us (1%)
    pallas_call x1, Pallas kernels, shards(): pl.pallas_call(body, name='step', out_shape=(jax.ShapeDtypeStruct((1024,...  53.5 us
    unnamed x7, local copies, waits for them, and re-layouts  3.55 us

profile of v1, /device:TPU:1, one launch (start us, length us, event | category | flops | bytes accessed | tf_op | source)
XLA Modules:
  0.0 57.7 jit_solution(10982149509965247290)
XLA Ops:
  0.6 53.5 %step.1 = (f32[1024,256]{1,0:T(8,128)}, bf16[128,256]{1,0:T(8,128)(2,1)}, f32[64,128]{1,0:T(8,128)}) custom-call(bf16[1,256,1024]{2,1,0:T(8,128)(2,1)} %ui.1, bf16[1,256,3584]{2,1,0:T(8,128)(2,1)} %gp.1, bf16[1,256,3584]{2,1,0:T(8,128)(2,1)} %up.1, bf16[1,256,3584]{2,1,0:T(8,128)(2,1)} %gh.1, bf16[1,256,1024]{2,1,0:T(8,128)(2,1)} %go.1, ...), custom_call_target="tpu_custom_call" | custom-call | tf_op jit(solution)/shard_map/step/pallas_call | solution.py:430
  54.1 0.0 copy-start
  54.2 0.0 copy-start.1
  54.2 2.3 %copy.17 = f32[1024,256]{1,0:T(8,128)} copy(f32[1024,256]{1,0:T(8,128)} %get-tuple-element.6) | data formatting | bytes 2097152
  56.5 0.0 copy-done
  56.5 0.6 %copy.18 = bf16[128,256]{1,0:T(8,128)(2,1)} copy(bf16[128,256]{1,0:T(8,128)(2,1)S(1)} %copy-done) | data formatting | bytes 131072
  57.1 0.0 copy-done.1
  57.1 0.6 %copy.19 = f32[64,128]{1,0:T(8,128)} copy(f32[64,128]{1,0:T(8,128)S(1)} %copy-done.1) | data formatting | bytes 65536
Async XLA Ops:
  54.1 2.3 %copy-start = (bf16[128,256]{1,0:T(8,128)(2,1)S(1)}, bf16[128,256]{1,0:T(8,128)(2,1)}, u32[]{:S(2)}) copy-start(bf16[128,256]{1,0:T(8,128)(2,1)} %get-tuple-element.7) | copy-start | bytes 196612
  54.2 2.9 %copy-start.1 = (f32[64,128]{1,0:T(8,128)S(1)}, f32[64,128]{1,0:T(8,128)}, u32[]{:S(2)}) copy-start(f32[64,128]{1,0:T(8,128)} %get-tuple-element.8) | copy-start | bytes 98308

commit v2 on v1

v2 whole, which is shorter than its diff:
```python
import math

import jax
import jax.numpy as jnp
from jax import lax
from jax.experimental import pallas as pl
from jax.experimental.pallas import tpu as pltpu
from jax.sharding import Mesh
from jax.sharding import PartitionSpec as P

GRP_DP = ("g", "y", "h", "c")
DP = ("y", "h", "c")
GX = ("g", "x")
NCH = 7
ROWS = 32
HI = lax.Precision.HIGHEST
F32 = jnp.float32
BF = jnp.bfloat16
NT = (((1,), (1,)), ((), ()))
TN = (((0,), (0,)), ((), ()))
MESH = pl.DeviceIdType.MESH

C_Z, C_Y, C_R, C_P = 0, 6, 22, 30
A_, FZ, FY, FK, TX, TZ, EZ, EY = 46, 58, 65, 68, 69, 72, 73, 76
SLOTS = 83


def dot_nt(a, b, precision=None):
    return lax.dot_general(a, b, NT, precision=precision, preferred_element_type=F32)


def body(
    ui, gp, up, gh, go, pui, puo, pdi, pdo, gram, can,
    fk_out, fd_out, mapped_out, scores_out,
    ui_v, gp_v, up_v, gh_v, go_v, pui_v, puo_v, pdi_v, pdo_v, gram_v,
    gu_b, hid_b, acc_ou, acc_id, gram_b,
    cf, a_in, a_out, ra_in, ra_out, fz, fown, fka, fd,
    pst, pown, rp, ts, town, rt, tq, rtq,
    es, res, ey, rey, r_v, k_v,
    ls, ss, rs, fds, fdr, ps, pr,
):
    g, y, h, c, x = (lax.axis_index(n) for n in ("g", "y", "h", "c", "x"))
    z = h * 2 + g
    oc = 1 - c
    og = 1 - g
    rem = lax.rem
    hp, hm, h2 = rem(h + 1, 4), rem(h + 3, 4), rem(h + 2, 4)
    yp, ym, y2 = rem(y + 1, 4), rem(y + 3, 4), rem(y + 2, 4)
    hk = (h, hm, hp, h2)
    yj = (y, ym, yp, y2)

    bar = pltpu.get_barrier_semaphore()
    near = [dict(y=yp), dict(y=ym), dict(h=hp), dict(h=hm), dict(g=og), dict(c=oc)]
    for r in range(1, 4):
        near += [dict(x=rem(x + r, 4)), dict(x=rem(x + r, 4), c=oc)]
    for dev in near:
        pl.semaphore_signal(bar, inc=1, device_id=dev, device_id_type=MESH)

    loads = []

    def load(src, dst):
        cp = pltpu.make_async_copy(src, dst, ls.at[len(loads)])
        cp.start()
        loads.append(cp)
        return cp

    def blk(yy, hh, cc):
        return (yy * 4 + hh) * 2 + cc

    own = blk(y, h, c)
    l_c = load(can, cf.at[own])
    l_in = [load(a, b) for a, b in ((pui, pui_v), (ui.at[0], ui_v), (pdo, pdo_v), (go.at[0], go_v))]
    l_p = [load(puo, puo_v), load(pdi, pdi_v)]
    l_ch = []
    for k in range(NCH):
        s = pl.ds(k * 512, 512)
        l_ch.append([load(a.at[0, :, s], b.at[k]) for a, b in ((gp, gp_v), (gh, gh_v), (up, up_v))])
    l_g = load(gram, gram_v)

    live = {}

    def send(src, dst, slot, **dev):
        cp = pltpu.make_async_remote_copy(
            src_ref=src, dst_ref=dst, send_sem=ss.at[slot], recv_sem=rs.at[slot],
            device_id=dev, device_id_type=MESH,
        )
        cp.start()
        live[slot] = cp

    def got(slot):
        live[slot].wait_recv()

    def chunk(k):
        for cp in l_ch[k]:
            cp.wait()

        def tile(i, _):
            rows = pl.ds(i * ROWS, ROWS)
            v = gp_v[k, rows, :].astype(F32)
            act = v / (1.0 + jnp.exp(-v))
            gu_b[rows, :] = (gh_v[k, rows, :].astype(F32) * act).astype(BF)
            hid_b[rows, :] = (act * up_v[k, rows, :].astype(F32)).astype(BF)
            return 0

        lax.fori_loop(0, 256 // ROWS, tile, 0)
        s = slice(k * 512, (k + 1) * 512)
        ou = dot_nt(puo_v[:, s], gu_b[...])
        idn = dot_nt(pdi_v[:, s], hid_b[...])
        if k == 0:
            acc_ou[...] = ou
            acc_id[...] = idn
        else:
            acc_ou[...] += ou
            acc_id[...] += idn

    half = (pl.ds(0, 16), pl.ds(16, 16))
    dirs = (yp, ym)

    def move(b, part, slot, **dev):
        ref = cf.at[b] if part is None else cf.at[b, half[part]]
        send(ref, ref, slot, **dev)

    def partner(j, k):
        move(blk(yj[j], hk[k], c), None, C_P + j * 4 + k, c=oc)

    def y_slot(d, k, part):
        return C_Y + (d * 4 + k) * 2 + part

    def spread(k, part, order=(0, 1)):
        b = blk(y, hk[k], c)
        for d in order:
            move(b, part, y_slot(d, k, part), y=dirs[d])

    def c_start():
        l_c.wait()
        move(own, 0, C_Z, h=hp)
        move(own, 1, C_Z + 2, h=hm)
        move(own, 0, y_slot(0, 0, 0), y=yp)
        move(own, 1, y_slot(1, 0, 1), y=ym)
        move(own, 1, C_Z + 1, h=hp)
        move(own, 0, C_Z + 3, h=hm)
        move(own, 1, y_slot(0, 0, 1), y=yp)
        move(own, 0, y_slot(1, 0, 0), y=ym)
        partner(0, 0)

    def c_z1():
        got(C_Z)
        move(blk(y, hm, c), 0, C_Z + 4, h=hp)
        spread(1, 0)
        got(C_Z + 2)
        move(blk(y, hp, c), 1, C_Z + 5, h=hm)
        spread(2, 1)

    def c_z2():
        got(C_Z + 1)
        spread(1, 1)
        partner(0, 1)
        got(C_Z + 3)
        spread(2, 0)
        partner(0, 2)

    def c_z3():
        got(C_Z + 4)
        spread(3, 0)
        got(C_Z + 5)
        spread(3, 1)
        partner(0, 3)

    def c_rel(k):
        got(y_slot(0, k, 0))
        move(blk(ym, hk[k], c), 0, C_R + k, y=yp)
        got(y_slot(1, k, 1))
        move(blk(yp, hk[k], c), 1, C_R + 4 + k, y=ym)

    def c_ydone(k):
        got(y_slot(0, k, 1))
        partner(1, k)
        got(y_slot(1, k, 0))
        partner(2, k)

    def c_y2(k):
        got(C_R + k)
        got(C_R + 4 + k)
        partner(3, k)

    def p_to(j, i):
        gq, xq = yj[j] // 2, 2 * rem(yj[j], 2) + i
        rel = rem(gq + g, 2) * 4 + rem(xq + 4 - x, 4)
        slot = jnp.maximum(rel - 1, 0)
        n = j * 2 + i
        cp = pltpu.make_async_remote_copy(
            src_ref=pst.at[n], dst_ref=rp.at[slot], send_sem=ps.at[n], recv_sem=pr.at[slot],
            device_id=dict(g=gq, x=xq), device_id_type=MESH,
        )
        return cp, rel

    def p_group(j):
        for k in range(4):
            got(C_P + j * 4 + k)
        for i in range(2):
            b = 2 * yj[j] + i
            prod = jnp.dot(cf[pl.ds(4 * b, 4)].reshape(128, 1024), gram_b[...], preferred_element_type=F32)
            pst[j * 2 + i] = prod.astype(BF)
            cp, rel = p_to(j, i)

            @pl.when(rel != 0)
            def _():
                cp.start()

            @pl.when(rel == 0)
            def _():
                pown[...] = prod

    for cp in l_in:
        cp.wait()
    iu = dot_nt(pui_v[...], ui_v[...])
    od = dot_nt(pdo_v[...], go_v[...])
    a_in[0] = iu.astype(BF)
    a_out[1] = od.reshape(4, 16, 256)
    for cp in l_p:
        cp.wait()
    chunk(0)
    pl.semaphore_wait(bar, len(near))
    c_start()

    def a_send(q, m_in, m_out):
        for r in range(1, 4):
            xp = rem(x + r, 4)
            send(a_in.at[m_in], ra_in.at[r - 1, m_in], A_ + q * 6 + 2 * (r - 1), x=xp)
            send(a_out.at[m_out, xp], ra_out.at[r - 1, m_out], A_ + q * 6 + 2 * (r - 1) + 1, x=xp)

    a_send(0, 0, 1)
    chunk(1)
    chunk(2)
    chunk(3)
    c_z1()
    c_rel(0)
    chunk(4)
    c_z2()
    chunk(5)
    chunk(6)
    idn = acc_id[...]
    ou = acc_ou[...]
    a_in[1] = idn.astype(BF)
    a_out[0] = ou.reshape(4, 16, 256)
    a_send(1, 1, 0)
    c_z3()
    c_ydone(0)
    c_rel(1)
    c_rel(2)
    l_g.wait()
    gram_b[...] = gram_v[...].astype(BF)
    for s in range(6):
        got(A_ + s)
    p_group(0)

    lane = lax.broadcasted_iota(jnp.int32, (64, 1024), 1)
    tile_m = jnp.where(lane % 64 == lax.broadcasted_iota(jnp.int32, (64, 1024), 0), 1.0, 0.0).astype(BF)
    lane16 = lax.broadcasted_iota(jnp.int32, (16, 1024), 1)
    mask16 = lane16 // 64 == lax.broadcasted_iota(jnp.int32, (16, 1024), 0)

    for s in range(6, 12):
        got(A_ + s)
    for m, mine in ((0, iu), (1, idn)):
        ins, outs = mine, a_out[m, x]
        for r in range(3):
            ins = ins + ra_in[r, m].astype(F32)
            outs = outs + ra_out[r, m]
        feat = dot_nt(outs, ins, HI) * (1.0 / 16.0)
        wide = jnp.dot(feat.astype(BF), tile_m, preferred_element_type=F32)
        row = jnp.sum(jnp.where(mask16, wide, 0.0), axis=0, keepdims=True)
        fz[pl.ds(z, 1), m * 1024 : (m + 1) * 1024] = row

    for r in range(1, 8):
        zz = rem(z + r, 8)
        send(fz.at[pl.ds(z, 1)], fz.at[pl.ds(z, 1)], FZ + r - 1, h=zz // 2, g=rem(zz, 2))
    c_ydone(1)
    c_ydone(2)
    c_rel(3)
    c_y2(0)
    c_y2(1)
    c_ydone(3)
    p_group(1)
    p_group(2)
    for r in range(7):
        got(FZ + r)
    fown[...] = fz[...].astype(BF)
    gl = pl.ds(pl.multiple_of(g * 1024, 1024), 1024)
    fka[y, c] = fown[:, gl]

    is_src = h // 2 == rem(x, 2)

    def fd_copies():
        remote, local = [], []
        for n in range(2):
            yt = x // 2 + 2 * n
            for r in range(4):
                for q, cc in enumerate((c, oc)):
                    i = n * 8 + r * 2 + q
                    lo = pl.multiple_of(n * 1024 + rem(h, 2) * 512 + cc * 256, 256)
                    piece = fown.at[:, pl.ds(lo, 256)]
                    cp = pltpu.make_async_remote_copy(
                        src_ref=piece, dst_ref=fd.at[y, c], send_sem=fds.at[i], recv_sem=fdr.at[y, c],
                        device_id=dict(y=yt, x=rem(x + r, 4), c=cc), device_id_type=MESH,
                    )
                    if r == 0 and q == 0:
                        remote.append((cp, yt != y))
                        local.append((pltpu.make_async_copy(piece, fd.at[y, c], fdr.at[y, c]), yt == y))
                    else:
                        remote.append((cp, None))
        return remote, local

    @pl.when(is_src)
    def _():
        remote, local = fd_copies()
        for cp, cond in remote:
            if cond is None:
                cp.start()
            else:
                pl.when(cond)(cp.start)
        for cp, cond in local:
            pl.when(cond)(cp.start)

    for r in range(1, 4):
        send(fka.at[y, c], fka.at[y, c], FY + r - 1, y=rem(y + r, 4))
    c_y2(2)
    c_y2(3)
    p_group(3)
    for r in range(3):
        got(FY + r)
    send(fka.at[:, c], fka.at[:, c], FK, c=oc)
    for yy in range(4):
        for cc in range(2):
            pltpu.make_async_copy(fd.at[yy, cc], fd.at[yy, cc], fdr.at[yy, cc]).wait()
    fd32 = fd[...].astype(F32).reshape(64, 256)
    fdb = fd32.astype(BF)
    fd_out[...] = fdb

    rr = pown[...]
    for s in range(7):
        pltpu.make_async_copy(rp.at[s], rp.at[s], pr.at[s]).wait()
        rr = rr + rp[s].astype(F32)
    r_v[...] = rr
    r_hi = rr.astype(BF)
    r_lo = (rr - r_hi.astype(F32)).astype(BF)
    s1 = dot_nt(fdb, r_hi) + dot_nt(fdb, r_lo)
    ey[...] = s1
    es[0] = s1.astype(BF)
    for r in range(1, 4):
        send(es.at[0], res.at[r - 1], EZ + r - 1, h=rem(h + r, 4))

    got(FK)
    fk = fka[...].astype(F32).reshape(64, 1024).astype(BF)
    fk_out[...] = fk
    ft = dot_nt(fk, cf[...].reshape(1024, 1024))
    fkk = dot_nt(fk, jnp.concatenate([fk, fk], axis=0))
    for b in range(8):
        town[b % 4, b // 4] = ft[:, b * 128 : (b + 1) * 128]
        ts[b % 4, b // 4] = ft[:, b * 128 : (b + 1) * 128].astype(BF)
    k_v[...] = fkk
    for b in range(4):
        ts[b, 2] = fkk.astype(BF)
    for r in range(1, 4):
        xp = rem(x + r, 4)
        send(ts.at[xp], rt.at[r - 1], TX + r - 1, x=xp)
    for r in range(3):
        got(TX + r)
    for q in range(2):
        acc = town[x, q]
        for r in range(3):
            acc = acc + rt[r, q].astype(F32)
        town[x, q] = acc
    acc = k_v[...]
    for r in range(3):
        acc = acc + rt[r, 2].astype(F32)
    k_v[...] = acc
    tq[0] = town[x, og].astype(BF)
    tq[1] = acc.astype(BF)
    send(tq, rtq, TZ, g=og)

    for r in range(3):
        got(EZ + r)
    acc = ey[...]
    for r in range(3):
        acc = acc + res[r].astype(F32)
    ey[...] = acc
    es[1] = acc.astype(BF)
    for r in range(1, 4):
        yt = rem(y + r, 4)
        send(es.at[1], rey.at[r - 1], EY + r - 1, y=yt)
        send(es.at[1], rey.at[r + 2], EY + r + 2, y=yt, c=oc)
    send(es.at[1], rey.at[6], EY + 6, c=oc)

    got(TZ)
    t_f = town[x, g] + rtq[0].astype(F32)
    k_f = (k_v[...] + rtq[1].astype(F32))[:, :64]
    norm = 1.0 / math.sqrt(8192.0)
    tf = lax.dot_general(t_f, fd32, TN, precision=HI, preferred_element_type=F32)
    mapped_out[...] = ((r_v[...] + tf * (1.0 / 64.0)) * norm).astype(BF)
    kt = jnp.dot(k_f, t_f, precision=HI, preferred_element_type=F32)

    acc = ey[...] + kt * (1.0 / 64.0)
    for s in range(7):
        got(EY + s)
        acc = acc + rey[s].astype(F32)
    scores_out[...] = acc * (1.0 / 8192.0)

    for cp in live.values():
        cp.wait_send()
    for j in range(4):
        for i in range(2):
            cp, rel = p_to(j, i)
            pl.when(rel != 0)(cp.wait_send)

    @pl.when(is_src)
    def _():
        for cp, cond in fd_copies()[0]:
            if cond is None:
                cp.wait_send()
            else:
                pl.when(cond)(cp.wait_send)


def finish(gram, fk, fd, mapped, scores, gram_out, mapped_out, scores_out, gin, gnew, sin, sout):
    def part(i):
        return pl.ds(i * 256, 256)

    ins = [pltpu.make_async_copy(gram.at[part(i)], gin.at[part(i)], sin.at[i]) for i in range(4)]
    outs = [pltpu.make_async_copy(gnew.at[part(i)], gram_out.at[part(i)], sout.at[i]) for i in range(4)]
    for cp in ins:
        cp.start()
    mapped_out[...] = mapped[...]
    for s in range(64):
        yy, cc, zz = s // 16, (s // 8) % 2, s % 8
        t = (zz % 2) * 32 + yy * 8 + (zz // 2) * 2 + cc
        scores_out[t : t + 1, :] = scores[s : s + 1, :]
    for i in range(4):
        add = lax.dot_general(fk[:, i * 256 : (i + 1) * 256], fd[...], TN, preferred_element_type=F32)
        ins[i].wait()
        gnew[part(i), :] = gin[part(i), :] + add * (1.0 / 64.0)
        outs[i].start()
    for cp in outs:
        cp.wait()


def shards(*args):
    any_ = pl.BlockSpec(memory_space=pl.ANY)
    vm = pl.BlockSpec(memory_space=pltpu.VMEM)
    V = pltpu.VMEM
    dma = pltpu.SemaphoreType.DMA
    S = jax.ShapeDtypeStruct
    scratch = [
        V((256, 1024), BF), V((NCH, 256, 512), BF), V((NCH, 256, 512), BF), V((NCH, 256, 512), BF),
        V((256, 1024), BF), V((64, 1024), BF), V((64, 3584), BF), V((64, 3584), BF), V((64, 1024), BF),
        V((1024, 256), F32),
        V((256, 512), BF), V((256, 512), BF), V((64, 256), F32), V((64, 256), F32), V((1024, 256), BF),
        V((32, 32, 1024), BF),
        V((2, 64, 256), BF), V((2, 4, 16, 256), F32), V((3, 2, 64, 256), BF), V((3, 2, 16, 256), F32),
        V((8, 2048), F32), V((8, 2048), BF), V((4, 2, 8, 1024), BF), V((4, 2, 8, 256), BF),
        V((8, 128, 256), BF), V((128, 256), F32), V((7, 128, 256), BF),
        V((4, 3, 64, 128), BF), V((4, 2, 64, 128), F32), V((3, 3, 64, 128), BF),
        V((2, 64, 128), BF), V((2, 64, 128), BF),
        V((2, 64, 128), BF), V((3, 64, 128), BF), V((64, 128), F32), V((7, 64, 128), BF),
        V((128, 256), F32), V((64, 128), F32),
        dma((40,)), dma((SLOTS,)), dma((SLOTS,)), dma((16,)), dma((4, 2)), dma((8,)), dma((7,)),
    ]
    gram = args[9]
    fk, fd, mapped, scores = pl.pallas_call(
        body,
        name="step",
        out_shape=(S((64, 1024), BF), S((64, 256), BF), S((128, 256), BF), S((64, 128), F32)),
        in_specs=[any_] * 11,
        out_specs=(vm,) * 4,
        scratch_shapes=scratch,
        compiler_params=pltpu.CompilerParams(collective_id=0, has_side_effects=True),
    )(*args)
    return pl.pallas_call(
        finish,
        name="finish",
        out_shape=(S((1024, 256), F32), S((128, 256), BF), S((64, 128), F32)),
        in_specs=[any_] + [vm] * 4,
        out_specs=(any_, vm, vm),
        scratch_shapes=[V((1024, 256), F32), V((1024, 256), F32), dma((4,)), dma((4,))],
    )(gram, fk, fd, mapped, scores)


def solution(mesh):
    finer = Mesh(mesh.devices.reshape(2, 4, 4, 2, 4), ("g", "y", "h", "c", "x"))
    in_specs = (P(GRP_DP, None, "x"),) * 5 + (P(None, "x"),) * 4 + (P(GX, DP), P(DP, GX))
    out_specs = (P(GX, DP), P(GX, DP), P(None, GX))
    return jax.shard_map(shards, mesh=finer, in_specs=in_specs, out_specs=out_specs, check_vma=False)
```

time: 57.8 us -> 54.7 us (0.946)
  local copies, waits for them, and re-layouts: 3.55 us -> 0 us
    unnamed x7 -> x0, local copies, waits for them, and re-layouts: 3.55 us -> none
    pallas_call x1 -> x2, Pallas kernels: 53.5 us -> 54 us  [the longest x1 50 us: shards(): pl.pallas_call(body, name='step', out_shape=(S((64, 1024), BF), S((64, 25...]
where the time goes in v2:
time: 54.7 us; the launch traced here: 54.6 us
  Pallas kernels  54 us (99%)
  between operations  0.64 us (1%)
    pallas_call x1, Pallas kernels, shards(): pl.pallas_call(body, name='step', out_shape=(S((64, 1024), BF), S((64, 25...  50 us
    pallas_call x1, Pallas kernels, shards(): pl.pallas_call(finish, name='finish', out_shape=(S((1024, 256), F32), S((...  4.03 us

profile of v2, /device:TPU:1, one launch (start us, length us, event | category | flops | bytes accessed | tf_op | source)
XLA Modules:
  0.0 54.6 jit_solution(3883796749712819856)
XLA Ops:
  0.6 50.0 %step.1 = (bf16[64,1024]{1,0:T(8,128)(2,1)}, bf16[64,256]{1,0:T(8,128)(2,1)}, bf16[128,256]{1,0:T(8,128)(2,1)}, f32[64,128]{1,0:T(8,128)}) custom-call(bf16[1,256,1024]{2,1,0:T(8,128)(2,1)} %ui.1, bf16[1,256,3584]{2,1,0:T(8,128)(2,1)} %gp.1, bf16[1,256,3584]{2,1,0:T(8,128)(2,1)} %up.1, bf16[1,256,3584]{2,1,0:T(8,128)(2,1)} %gh.1, bf16[1,256,1024]{2,1,0:T(8,128)(2,1)} %go.1, ...), custom_call_target="tpu_custom_call" | custom-call | tf_op jit(solution)/shard_map/step/pallas_call | solution.py:468
  50.6 4.0 %finish.1 = (f32[1024,256]{1,0:T(8,128)}, bf16[128,256]{1,0:T(8,128)(2,1)}, f32[64,128]{1,0:T(8,128)}) custom-call(f32[1024,256]{1,0:T(8,128)} %gram.3, bf16[64,1024]{1,0:T(8,128)(2,1)} %get-tuple-element.7.fk, bf16[64,256]{1,0:T(8,128)(2,1)} %get-tuple-element.8.fd, bf16[128,256]{1,0:T(8,128)(2,1)} %get-tuple-element.9.mapped, ...), custom_call_target="tpu_custom_call" | custom-call | tf_op jit(solution)/shard_map/finish/pallas_call | solution.py:477
